TPU v7x, 128 devices: a whole 4x4x4 slice. The times are simulated.
128 devices in a mesh: dp: 64 (over y_hi, z, x, core), col: 2 (over y_lo).
Axes of the slice: x: 4, y: 4 (y_hi: 2, y_lo: 2; y = y_hi * 2 + y_lo), z: 4, core: 2. Of those that a mesh axis runs over, the one named last changes fastest.
Arguments:
- tokens: bfloat16 [8192, 2048], P('dp'), may hold values from -6 to 6
- routes: int32 [8192, 8], P('dp'), may hold values from 0 to 127, all different within a row; in each aligned block of 128 rows (0 to 127, 128 to 255, ...) at most 12 rows name the same one
- probs: float32 [8192, 8], P('dp'), may hold values from 0.1 to 1
- w_gate: bfloat16 [128, 2048, 768], P('dp', None, 'col'), may hold values from -0.125 to 0.125
- w_up: bfloat16 [128, 2048, 768], P('dp', None, 'col'), may hold values from -0.125 to 0.125
- w_down: bfloat16 [128, 768, 2048], P('dp', 'col'), may hold values from -0.21875 to 0.21875
- cotangent: bfloat16 [8192, 2048], P('dp', 'col'), may hold values from -6 to 6
Outputs:
- mixed: bfloat16 [8192, 2048], P('dp', 'col')
- grad_tokens: bfloat16 [8192, 2048], P('dp', 'col')
- grad_probs: float32 [8192, 8], P('dp')
- grad_gate: bfloat16 [128, 2048, 768], P('dp', None, 'col')
- grad_up: bfloat16 [128, 2048, 768], P('dp', None, 'col')
- grad_down: bfloat16 [128, 768, 2048], P('dp', 'col')
Inputs may be any that keep to these rules, and one draw needn't show every extreme that they name: `routes`: each token names 8 different experts. Among the 128 tokens of one index of dp, no expert is named by more than 12 of them, a bound that some block reaches.
All inputs are finite; a program needn't handle non-finite values.
Results may differ from a plain program's by a relative error of at most 0.0064.
Values may be sent and summed in bfloat16 or wider, within the bound.
A program may use at most 192 MiB of HBM per device.

v0:
```python
import jax
import jax.numpy as jnp
from jax import lax
from jax.sharding import PartitionSpec as P


def body(tokens, routes, probs, w_gate, w_up, w_down, cotangent):
    tok_count, width = tokens.shape
    top_count = routes.shape[1]
    owners = lax.axis_size("dp")
    local_experts = w_gate.shape[0]
    experts = local_experts * owners
    slot_cap = 3 * tok_count * top_count // (2 * experts)
    half_width = width // lax.axis_size("col")
    flat_routes = routes.reshape(-1)
    expert_ids = jnp.arange(experts, dtype=jnp.int32)
    onehot = (flat_routes[:, None] == expert_ids[None, :]).astype(jnp.int32)
    before = jnp.cumsum(onehot, axis=0) - onehot
    slot_index = jnp.sum(before * onehot, axis=1)
    flat_index = flat_routes * slot_cap + slot_index

    def scatter_rows(row_pairs):
        buffer = jnp.zeros((experts * slot_cap, row_pairs.shape[1]), row_pairs.dtype)
        buffer = buffer.at[flat_index].set(row_pairs)
        return buffer.reshape(owners, local_experts * slot_cap, row_pairs.shape[1])

    def send_whole(row_pairs):
        return lax.all_to_all(
            scatter_rows(row_pairs), "dp", split_axis=0, concat_axis=0, tiled=True
        )

    def send_back(partial_value):
        summed = lax.psum_scatter(partial_value, "col", scatter_dimension=2, tiled=True).astype(
            jnp.bfloat16
        )
        returned = lax.all_to_all(summed, "dp", split_axis=0, concat_axis=0, tiled=True)
        return returned.reshape(experts * slot_cap, half_width)[flat_index].reshape(
            tok_count, top_count, half_width
        )

    arrived_rows = send_whole(jnp.repeat(tokens, top_count, axis=0))
    row_block = arrived_rows.reshape(owners, local_experts, slot_cap, width)
    gate_acts = jnp.einsum("slcd,ldh->slch", row_block, w_gate, preferred_element_type=jnp.float32)
    up_acts = jnp.einsum("slcd,ldh->slch", row_block, w_up, preferred_element_type=jnp.float32)
    sigmoid_g = jax.nn.sigmoid(gate_acts)
    silu_g = gate_acts * sigmoid_g
    hidden = (silu_g * up_acts).astype(jnp.bfloat16)
    out_partial = jnp.einsum("slch,lhd->slcd", hidden, w_down, preferred_element_type=jnp.float32)
    picked_out = send_back(out_partial.reshape(owners, local_experts * slot_cap, width))
    picked_wide = picked_out.astype(jnp.float32)
    mixed = jnp.sum(probs[:, :, None] * picked_wide, axis=1).astype(jnp.bfloat16)
    cot_wide = cotangent.astype(jnp.float32)
    prob_part = jnp.sum(cot_wide[:, None, :] * picked_wide, axis=2)
    full_cot = lax.all_gather(cotangent, "col", axis=1, tiled=True)
    scaled_full = (probs[:, :, None] * full_cot.astype(jnp.float32)[:, None, :]).astype(
        jnp.bfloat16
    )
    arrived_cot = send_whole(scaled_full.reshape(tok_count * top_count, width))
    d_out = arrived_cot.reshape(owners, local_experts, slot_cap, width)
    grad_down = jnp.einsum(
        "slch,slcd->lhd", hidden, d_out, preferred_element_type=jnp.float32
    ).astype(jnp.bfloat16)
    d_hidden = jnp.einsum("slcd,lhd->slch", d_out, w_down, preferred_element_type=jnp.float32)
    d_gate = (d_hidden * up_acts * sigmoid_g * (1.0 + gate_acts * (1.0 - sigmoid_g))).astype(
        jnp.bfloat16
    )
    d_up = (d_hidden * silu_g).astype(jnp.bfloat16)
    grad_gate = jnp.einsum(
        "slcd,slch->ldh", row_block, d_gate, preferred_element_type=jnp.float32
    ).astype(jnp.bfloat16)
    grad_up = jnp.einsum(
        "slcd,slch->ldh", row_block, d_up, preferred_element_type=jnp.float32
    ).astype(jnp.bfloat16)
    d_partial = jnp.einsum(
        "slch,ldh->slcd", d_gate, w_gate, preferred_element_type=jnp.float32
    ) + jnp.einsum("slch,ldh->slcd", d_up, w_up, preferred_element_type=jnp.float32)
    picked_grad = send_back(d_partial.reshape(owners, local_experts * slot_cap, width))
    grad_tokens = jnp.sum(picked_grad.astype(jnp.float32), axis=1).astype(jnp.bfloat16)
    grad_probs = lax.psum(prob_part, "col")
    return (mixed, grad_tokens, grad_probs, grad_gate, grad_up, grad_down)


def solution(mesh):
    return jax.shard_map(
        body,
        mesh=mesh,
        in_specs=(
            P("dp", None),
            P("dp", None),
            P("dp", None),
            P("dp", None, "col"),
            P("dp", None, "col"),
            P("dp", "col", None),
            P("dp", "col"),
        ),
        out_specs=(
            P("dp", "col"),
            P("dp", "col"),
            P("dp", None),
            P("dp", None, "col"),
            P("dp", None, "col"),
            P("dp", "col", None),
        ),
        check_vma=False,
    )
```

profile of v0, /device:TPU:10, one launch (start us, length us, event | category | flops | bytes accessed | tf_op | source)
XLA Modules:
  0.0 687.5 jit_solution(13827045977689101927)
XLA Ops:
  7.2 0.8 broadcast_multiply_fusion
  8.0 0.9 copy.29
  8.9 0.1 eq.29
  9.1 0.1 copy.28
  9.2 0.1 mul.81
  9.3 0.1 copy.31
  9.4 0.2 fusion.34
  9.6 0.8 copy-done.8
  10.4 1.1 broadcast_add_fusion
  11.5 0.1 copy.32
  11.6 0.4 fusion.33
  12.0 10.6 %scatter_custom_fusion = bf16[1536,2048]{1,0:T(8,128)(2,1)} fusion(s32[1024]{0:T(1024)S(1)} %bitcast.136, bf16[]{:T(256)} %constant.6.clone.1, bf16[128,2048]{1,0:T(8,128)(2,1)} %param.7), kind=kCustom, calls=%fused_computation.15 | custom fusion | bytes 6815746 | tf_op jit(solution)/shard_map/scatter | solution.py:24
  22.6 10.9 %all-to-all-start = ((bf16[64,24,2048]{2,1,0:T(8,128)(2,1)}), bf16[64,24,2048]{2,1,0:T(8,128)(2,1)}, u32[]{:S(2)}, u32[]{:S(2)}) async-start(bf16[64,24,2048]{2,1,0:T(8,128)(2,1)} %bitcast.126), calls=%async_computation | async-start | bytes 12582912 | tf_op jit(solution)/shard_map/all_to_all | solution.py:28
  33.5 0.1 copy.27
  33.6 0.1 mul.86
  33.7 87.4 %all_gather.3 = bf16[128,2048]{1,0:T(8,128)(2,1)S(1)} all-gather(bf16[128,1024]{1,0:T(8,128)(2,1)S(1)} %copy-done.11), channel_id=1, replica_groups=mesh['dp'=64,'col'=2] {'col'}, dimensions={1}, use_global_device_ids=true | all-gather | bytes 786432 | tf_op jit(solution)/shard_map/all_gather | solution.py:54
  121.1 1.1 convert_element_type.63
  122.2 11.0 %scatter_custom_fusion.1 = bf16[1536,2048]{1,0:T(8,128)(2,1)} fusion(s32[1024]{0:T(1024)S(1)} %bitcast.137, f32[128,2048]{1,0:T(8,128)} %convert_element_type.63, f32[1024]{0:T(1024)S(1)} %mul.86, bf16[]{:T(256)} %constant.6.clone.1), kind=kCustom, calls=%fused_computation.14 | custom fusion | flops 4194304 | bytes 7344130 | tf_op jit(solution)/shard_map/scatter | solution.py:24
  133.2 10.4 %all-to-all-start.2 = ((bf16[64,24,2048]{2,1,0:T(8,128)(2,1)}), bf16[64,24,2048]{2,1,0:T(8,128)(2,1)}, u32[]{:S(2)}, u32[]{:S(2)}) async-start(bf16[64,24,2048]{2,1,0:T(8,128)(2,1)} %bitcast.125), calls=%async_computation.3 | async-start | bytes 12582912 | tf_op jit(solution)/shard_map/all_to_all | solution.py:28
  143.6 0.2 reduce-scatter.5.cloned.1.call-start
  143.9 6.4 copy.33
  150.3 4.8 fusion.10
  155.1 4.8 fusion.14
  159.9 66.7 %all-to-all-done.2 = bf16[64,24,2048]{2,1,0:T(8,128)(2,1)} async-done(((bf16[64,24,2048]{2,1,0:T(8,128)(2,1)}), bf16[64,24,2048]{2,1,0:T(8,128)(2,1)}, u32[]{:S(2)}, u32[]{:S(2)}) %all-to-all-start.2) | async-done | bytes 6291488 | tf_op jit(solution)/shard_map/all_to_all | solution.py:28
  226.7 6.4 copy.36
  233.1 6.0 fusion.25
  239.1 4.9 fusion.12
  244.0 7.7 %convolution_add_fusion = f32[2,64,12,2048]{3,1,2,0:T(8,128)} fusion(f32[2,64,12,2048]{3,1,2,0:T(8,128)S(1)} %fusion.12, bf16[64,2,12,384]{3,0,2,1:T(8,128)(2,1)} %get-tuple-element.14, bf16[2,2048,384]{2,1,0:T(8,128)(2,1)S(1)} %copy-done.7), kind=kOutput, calls=%fused_computation.9 | convolution fusion | flops 2419064832 | bytes 29491200 | tf_op jit(solution)/shard_map/slch,ldh->slcd/dot_general | solution.py:76
  251.8 16.4 %copy.37 = f32[64,24,2048]{2,1,0:T(8,128)} copy(f32[64,24,2048]{2,0,1:T(8,128)} %bitcast.124) | data formatting | bytes 25165824 | tf_op jit(solution)/shard_map/reshape | solution.py:77
  268.2 7.9 %fusion.18 = f32[2,64,12,2048]{3,1,2,0:T(8,128)} fusion(bf16[64,2,12,384]{3,0,2,1:T(8,128)(2,1)} %get-tuple-element.16, bf16[2,384,2048]{2,1,0:T(8,128)(2,1)S(1)} %copy-done), kind=kOutput, calls=%fused_computation.28 | convolution fusion | flops 2415919104 | bytes 16908288 | tf_op jit(solution)/shard_map/slch,lhd->slcd/dot_general | solution.py:48
  276.2 17.3 %copy.34 = f32[64,24,2048]{2,1,0:T(8,128)} copy(f32[64,24,2048]{2,0,1:T(8,128)} %bitcast.123) | data formatting | bytes 25165824 | tf_op jit(solution)/shard_map/reshape | solution.py:49
  293.5 123.5 %reduce-scatter.5.cloned.1.call-done = f32[64,24,1024]{2,1,0:T(8,128)} async-done(((f32[64,24,2048]{2,1,0:T(8,128)}), f32[64,24,1024]{2,1,0:T(8,128)}) %reduce-scatter.5.cloned.1.call-update) | async-done | bytes 6291472 | tf_op jit(solution)/shard_map/reduce_scatter | solution.py:33
  417.1 4.9 convert_element_type.67
  422.0 9.8 %all-to-all-start.3 = ((bf16[64,24,1024]{2,1,0:T(8,128)(2,1)}), bf16[64,24,1024]{2,1,0:T(8,128)(2,1)S(1)}, u32[]{:S(2)}, u32[]{:S(2)}) async-start(bf16[64,24,1024]{2,1,0:T(8,128)(2,1)} %convert_element_type.67), calls=%async_computation.5 | async-start | bytes 6291456 | tf_op jit(solution)/shard_map/all_to_all | solution.py:36
  431.8 0.8 convert_element_type.68
  432.7 170.9 %reduce-scatter.3.cloned.1.call-done = f32[64,24,1024]{2,1,0:T(8,128)} async-done(((f32[64,24,2048]{2,1,0:T(8,128)}), f32[64,24,1024]{2,1,0:T(8,128)}) %reduce-scatter.3.cloned.1.call-update) | async-done | bytes 6291472 | tf_op jit(solution)/shard_map/reduce_scatter | solution.py:33
  603.6 4.9 convert_element_type.59
  608.5 7.9 %all-to-all-start.1 = ((bf16[64,24,1024]{2,1,0:T(8,128)(2,1)}), bf16[64,24,1024]{2,1,0:T(8,128)(2,1)}, u32[]{:S(2)}, u32[]{:S(2)}) async-start(bf16[64,24,1024]{2,1,0:T(8,128)(2,1)} %convert_element_type.59), calls=%async_computation.2 | async-start | bytes 6291456 | tf_op jit(solution)/shard_map/all_to_all | solution.py:36
  616.5 7.6 %bitcast_convert_fusion = bf16[2,384,2048]{2,1,0:T(8,128)(2,1)} fusion(bf16[64,2,12,384]{3,0,2,1:T(8,128)(2,1)} %get-tuple-element.16, bf16[64,2,12,2048]{3,0,2,1:T(8,128)(2,1)} %bitcast.134), kind=kOutput, calls=%fused_computation.6 | convolution fusion | flops 2417491968 | bytes 10616832 | tf_op jit(solution)/shard_map/slch,slcd->lhd/dot_general | solution.py:60
  624.1 8.1 %bitcast_convert_fusion.1 = bf16[2,2048,384]{2,1,0:T(8,128)(2,1)} fusion(bf16[64,2,12,2048]{3,0,2,1:T(8,128)(2,1)} %bitcast.129, bf16[64,2,12,384]{3,0,2,1:T(8,128)(2,1)S(1)} %copy-done.10), kind=kOutput, calls=%fused_computation.7 | convolution fusion | flops 2417491968 | bytes 10616832 | tf_op jit(solution)/shard_map/slcd,slch->ldh/dot_general | solution.py:71
  632.2 4.9 bitcast_convert_fusion.2
  637.1 5.4 gather_fusion.1
  642.5 3.7 bitcast_reduce_fusion
  646.2 11.5 %all-to-all-done.1 = bf16[64,24,1024]{2,1,0:T(8,128)(2,1)} async-done(((bf16[64,24,1024]{2,1,0:T(8,128)(2,1)}), bf16[64,24,1024]{2,1,0:T(8,128)(2,1)}, u32[]{:S(2)}, u32[]{:S(2)}) %all-to-all-start.1) | async-done | bytes 3145760 | tf_op jit(solution)/shard_map/all_to_all | solution.py:36
  657.7 8.5 %gather_fusion = bf16[1024,1024]{1,0:T(8,128)(2,1)} fusion(bf16[1536,1024]{1,0:T(8,128)(2,1)} %bitcast.18, s32[1024]{0:T(1024)S(1)} %broadcast_clamp_fusion), kind=kCustom, calls=%fused_computation | custom fusion | bytes 4198400 | tf_op jit(solution)/shard_map/gather | solution.py:37
  666.2 4.1 fusion.2
  670.2 9.6 %psum.7 = f32[128,8]{1,0:T(8,128)S(1)} all-reduce(f32[128,8]{1,0:T(8,128)S(1)} %get-tuple-element.12), channel_id=1, replica_groups=mesh['dp'=64,'col'=2] {'col'}, use_global_device_ids=true, to_apply=%region_10.11 | all-reduce | flops 1024 | bytes 8192 | tf_op jit(solution)/shard_map/psum | solution.py:79
  679.8 0.7 copy.38
  (45 shorter events, 0.3 us)
Async XLA Ops:
  7.2 225.9 %copy-start = (bf16[2,384,2048]{2,1,0:T(8,128)(2,1)S(1)}, bf16[2,384,2048]{2,1,0:T(8,128)(2,1)}, u32[]{:S(2)}) copy-start(bf16[2,384,2048]{2,1,0:T(8,128)(2,1)} %param.12) | copy-start | bytes 9437188
  9.6 0.8 copy-start.8
  22.6 10.9 %copy-start.12 = (f32[128,8]{0,1:T(8,128)S(1)}, f32[128,8]{0,1:T(8,128)}, u32[]{:S(2)}) copy-start(f32[128,8]{0,1:T(8,128)} %param.9) | copy-start | bytes 12292
  22.6 11.1 %copy-start.11 = (bf16[128,1024]{1,0:T(8,128)(2,1)S(1)}, bf16[128,1024]{1,0:T(8,128)(2,1)}, u32[]{:S(2)}) copy-start(bf16[128,1024]{1,0:T(8,128)(2,1)} %param.13) | copy-start | bytes 786436
  22.6 110.6 %all-to-all-start = ((bf16[64,24,2048]{2,1,0:T(8,128)(2,1)}), bf16[64,24,2048]{2,1,0:T(8,128)(2,1)}, u32[]{:S(2)}, u32[]{:S(2)}) async-start(bf16[64,24,2048]{2,1,0:T(8,128)(2,1)} %bitcast.126), calls=%async_computation | async-start | bytes 12582912 | tf_op jit(solution)/shard_map/all_to_all | solution.py:28
  133.2 93.5 %all-to-all-start.2 = ((bf16[64,24,2048]{2,1,0:T(8,128)(2,1)}), bf16[64,24,2048]{2,1,0:T(8,128)(2,1)}, u32[]{:S(2)}, u32[]{:S(2)}) async-start(bf16[64,24,2048]{2,1,0:T(8,128)(2,1)} %bitcast.125), calls=%async_computation.3 | async-start | bytes 12582912 | tf_op jit(solution)/shard_map/all_to_all | solution.py:28
  143.6 273.4 %reduce-scatter.5.cloned.1.call-start = ((), (), s32[]{:S(2)}) async-start(), calls=%async_computation.7 | async-start | bytes 18874368 | tf_op jit(solution)/shard_map/reduce_scatter | solution.py:33
  143.9 6.4 copy-start.6
  150.3 4.8 copy-start.2
  150.3 4.8 copy-start.4
  226.7 6.4 copy-start.13
  226.7 6.4 copy-start.14
  233.1 6.1 copy-start.3
  233.1 6.0 copy-start.5
  239.1 4.9 copy-start.7
  268.2 335.4 %reduce-scatter.3.cloned.1.call-start = ((), (), s32[]{:S(2)}) async-start(), calls=%async_computation.6 | async-start | bytes 18874368 | tf_op jit(solution)/shard_map/reduce_scatter | solution.py:33
  422.0 186.5 %all-to-all-start.3 = ((bf16[64,24,1024]{2,1,0:T(8,128)(2,1)}), bf16[64,24,1024]{2,1,0:T(8,128)(2,1)S(1)}, u32[]{:S(2)}, u32[]{:S(2)}) async-start(bf16[64,24,1024]{2,1,0:T(8,128)(2,1)} %convert_element_type.67), calls=%async_computation.5 | async-start | bytes 6291456 | tf_op jit(solution)/shard_map/all_to_all | solution.py:36
  608.5 49.1 %all-to-all-start.1 = ((bf16[64,24,1024]{2,1,0:T(8,128)(2,1)}), bf16[64,24,1024]{2,1,0:T(8,128)(2,1)}, u32[]{:S(2)}, u32[]{:S(2)}) async-start(bf16[64,24,1024]{2,1,0:T(8,128)(2,1)} %convert_element_type.59), calls=%async_computation.2 | async-start | bytes 6291456 | tf_op jit(solution)/shard_map/all_to_all | solution.py:36
  616.5 7.6 %copy-start.10 = (bf16[64,2,12,384]{3,0,2,1:T(8,128)(2,1)S(1)}, bf16[64,2,12,384]{3,0,2,1:T(8,128)(2,1)}, u32[]{:S(2)}) copy-start(bf16[64,2,12,384]{3,0,2,1:T(8,128)(2,1)} %get-tuple-element.14) | copy-start | bytes 3538948
  616.5 15.7 %slice-start = ((s8[6291456]{0:T(1024)(128)(4,1)}), s8[4194304]{0:T(1024)(128)(4,1)S(1)}, s32[]{:S(2)}) async-start(s8[6291456]{0:T(1024)(128)(4,1)} %bitcast.130), calls=%async_computation.8 | async-start | bytes 8388608
  624.1 8.1 %slice-start.1 = ((s8[6291456]{0:T(1024)(128)(4,1)}), s8[2097152]{0:T(1024)(128)(4,1)S(1)}, s32[]{:S(2)}) async-start(s8[6291456]{0:T(1024)(128)(4,1)} %bitcast.130), calls=%async_computation.9 | async-start | bytes 4194304
  624.1 8.1 %copy-start.9 = (bf16[64,2,12,384]{3,0,2,1:T(8,128)(2,1)S(1)}, bf16[64,2,12,384]{3,0,2,1:T(8,128)(2,1)}, u32[]{:S(2)}) copy-start(bf16[64,2,12,384]{3,0,2,1:T(8,128)(2,1)} %get-tuple-element.15) | copy-start | bytes 3538948
  657.7 22.8 %copy-start.1 = (bf16[2,384,2048]{2,1,0:T(8,128)(2,1)S(1)}, bf16[2,384,2048]{2,1,0:T(8,128)(2,1)}, u32[]{:S(2)}) copy-start(bf16[2,384,2048]{2,1,0:T(8,128)(2,1)} %param.12) | copy-start | bytes 9437188
Sparse Core Ops, SparseCore 0:
  268.3 148.7 reduce-scatter.4
  419.5 184.0 reduce-scatter.2
where the time goes:
time: 694 us; the launch traced here: 688 us
  waiting for transfers between devices  373 us (54%)
  blocking collectives  96.9 us (14%)
  local copies, waits for them, and re-layouts  74.1 us (11%)
  matrix products  56.8 us (8%)
  starting transfers between devices  39.3 us (6%)
  other arithmetic  33.1 us (5%)
  between operations  14.5 us (2%)
    reduce_scatter x2, waiting for transfers between devices, send_back(): lax.psum_scatter(partial_value, 'col', scatter_dimension=2, tiled=True)  294 us
    all_gather x1, blocking collectives, body(): full_cot = lax.all_gather(cotangent, 'col', axis=1, tiled=True)  87.4 us
    all_to_all x2, waiting for transfers between devices, send_whole(): lax.all_to_all(scatter_rows(row_pairs), 'dp', split_axis=0, concat_axis=0...  66.7 us
    all_to_all x2, starting transfers between devices, send_whole(): lax.all_to_all(scatter_rows(row_pairs), 'dp', split_axis=0, concat_axis=0...  21.3 us
    all_to_all x2, starting transfers between devices, send_back(): lax.all_to_all(summed, 'dp', split_axis=0, concat_axis=0, tiled=True)  17.7 us
    reshape x1, local copies, waits for them, and re-layouts, body(): out_partial.reshape(owners, local_experts * slot_cap, width)  17.3 us
    reshape x1, local copies, waits for them, and re-layouts, body(): d_partial.reshape(owners, local_experts * slot_cap, width)  16.4 us
  transfers between devices with their start and end apart: 6, of which 4 were waited for; matrix products, arithmetic and copies ran while one was open for 14% of the time, Pallas kernels for 0%

commit v1 on v0

--- a/solution.py
+++ b/solution.py
@@ -51,7 +51,9 @@
     mixed = jnp.sum(probs[:, :, None] * picked_wide, axis=1).astype(jnp.bfloat16)
     cot_wide = cotangent.astype(jnp.float32)
     prob_part = jnp.sum(cot_wide[:, None, :] * picked_wide, axis=2)
-    full_cot = lax.all_gather(cotangent, "col", axis=1, tiled=True)
+    full_cot = jnp.concatenate(
+        lax.all_to_all(jnp.stack([cotangent] * lax.axis_size("col")), "col", 0, 0), axis=1
+    )
     scaled_full = (probs[:, :, None] * full_cot.astype(jnp.float32)[:, None, :]).astype(
         jnp.bfloat16
     )

time: 694 us -> 685 us (0.987)
  blocking collectives: 96.9 us -> 9.55 us
  waiting for transfers between devices: 373 us -> 442 us
    all_gather x1 -> x0, blocking collectives: 87.4 us -> none  [body(): full_cot = lax.all_gather(cotangent, 'col', axis=1, tiled=True)]
    all_to_all x2, waiting for transfers between devices: 66.7 us -> 134 us  [send_whole(): lax.all_to_all(scatter_rows(row_pairs), 'dp', split_axis=0, concat_axis=0...]
  transfers between devices with their start and end apart: 6 -> 7, of which waited for: 4 -> 5; matrix products, arithmetic and copies ran while one was open for 14% -> 16% of each run, Pallas kernels for 0% -> 0%
where the time goes in v1:
time: 685 us; the launch traced here: 678 us
  waiting for transfers between devices  442 us (65%)
  local copies, waits for them, and re-layouts  76.8 us (11%)
  matrix products  57 us (8%)
  starting transfers between devices  43.4 us (6%)
  other arithmetic  34.8 us (5%)
  between operations  14.5 us (2%)
  blocking collectives  9.55 us (1%)
    reduce_scatter x2, waiting for transfers between devices, send_back(): lax.psum_scatter(partial_value, 'col', scatter_dimension=2, tiled=True)  297 us
    all_to_all x2, waiting for transfers between devices, send_whole(): lax.all_to_all(scatter_rows(row_pairs), 'dp', split_axis=0, concat_axis=0...  134 us
    all_to_all x2, starting transfers between devices, send_whole(): lax.all_to_all(scatter_rows(row_pairs), 'dp', split_axis=0, concat_axis=0...  20.6 us
    all_to_all x2, starting transfers between devices, send_back(): lax.all_to_all(summed, 'dp', split_axis=0, concat_axis=0, tiled=True)  17.9 us
    reshape x1, local copies, waits for them, and re-layouts, body(): d_partial.reshape(owners, local_experts * slot_cap, width)  16.4 us
    reshape x1, local copies, waits for them, and re-layouts, body(): out_partial.reshape(owners, local_experts * slot_cap, width)  16.3 us
    gather x2, local copies, waits for them, and re-layouts, send_back(): returned.reshape(experts * slot_cap, half_width)[flat_index]  13.8 us
  transfers between devices with their start and end apart: 7, of which 5 were waited for; matrix products, arithmetic and copies ran while one was open for 16% of the time, Pallas kernels for 0%

profile of v1, /device:TPU:10, one launch (start us, length us, event | category | flops | bytes accessed | tf_op | source)
XLA Modules:
  0.0 678.1 jit_solution(123122084829586388)
XLA Ops:
  7.2 1.3 copy.38
  8.5 0.8 pad_maximum_fusion
  9.3 4.6 all-to-all-start.2
  13.9 0.7 broadcast_multiply_fusion
  14.6 0.8 copy.31
  15.6 0.1 copy.33
  15.7 0.2 fusion.34
  15.9 0.8 copy-done.8
  16.7 1.1 broadcast_add_fusion
  17.8 0.1 copy.34
  17.9 0.4 fusion.33
  18.3 0.1 copy.30
  18.5 10.6 %scatter_custom_fusion = bf16[1536,2048]{1,0:T(8,128)(2,1)} fusion(s32[1024]{0:T(1024)S(1)} %bitcast.142, bf16[]{:T(256)} %constant.6.clone.1, bf16[128,2048]{1,0:T(8,128)(2,1)} %param.7), kind=kCustom, calls=%fused_computation.15 | custom fusion | bytes 6815746 | tf_op jit(solution)/shard_map/scatter | solution.py:24
  29.1 11.8 %all-to-all-start = ((bf16[64,24,2048]{2,1,0:T(8,128)(2,1)}), bf16[64,24,2048]{2,1,0:T(8,128)(2,1)}, u32[]{:S(2)}, u32[]{:S(2)}) async-start(bf16[64,24,2048]{2,1,0:T(8,128)(2,1)} %bitcast.129), calls=%async_computation | async-start | bytes 12582912 | tf_op jit(solution)/shard_map/all_to_all | solution.py:28
  41.2 2.1 convert_element_type.86
  43.2 2.5 copy.39
  45.8 11.0 %scatter_custom_fusion.1 = bf16[1536,2048]{1,0:T(8,128)(2,1)} fusion(s32[1024]{0:T(1024)S(1)} %bitcast.143, f32[128,2048]{1,0:T(8,128)} %copy.39, f32[1024]{0:T(1024)S(1)} %mul.86, bf16[]{:T(256)} %constant.6.clone.1), kind=kCustom, calls=%fused_computation.14 | custom fusion | flops 4194304 | bytes 7344130 | tf_op jit(solution)/shard_map/scatter | solution.py:24
  56.8 66.8 %all-to-all-done = bf16[64,24,2048]{2,1,0:T(8,128)(2,1)} async-done(((bf16[64,24,2048]{2,1,0:T(8,128)(2,1)}), bf16[64,24,2048]{2,1,0:T(8,128)(2,1)}, u32[]{:S(2)}, u32[]{:S(2)}) %all-to-all-start) | async-done | bytes 6291488 | tf_op jit(solution)/shard_map/all_to_all | solution.py:28
  123.6 8.8 %all-to-all-start.3 = ((bf16[64,24,2048]{2,1,0:T(8,128)(2,1)}), bf16[64,24,2048]{2,1,0:T(8,128)(2,1)}, u32[]{:S(2)}, u32[]{:S(2)}) async-start(bf16[64,24,2048]{2,1,0:T(8,128)(2,1)} %bitcast.130), calls=%async_computation.4 | async-start | bytes 12582912 | tf_op jit(solution)/shard_map/all_to_all | solution.py:28
  132.4 0.2 reduce-scatter.5.cloned.1.call-start
  132.7 6.4 copy.35
  139.1 4.8 fusion.10
  143.9 4.8 fusion.14
  148.7 66.7 %all-to-all-done.3 = bf16[64,24,2048]{2,1,0:T(8,128)(2,1)} async-done(((bf16[64,24,2048]{2,1,0:T(8,128)(2,1)}), bf16[64,24,2048]{2,1,0:T(8,128)(2,1)}, u32[]{:S(2)}, u32[]{:S(2)}) %all-to-all-start.3) | async-done | bytes 6291488 | tf_op jit(solution)/shard_map/all_to_all | solution.py:28
  215.5 6.4 copy.40
  221.9 6.0 fusion.25
  227.9 4.9 fusion.12
  232.8 7.8 %convolution_add_fusion = f32[2,64,12,2048]{3,1,2,0:T(8,128)} fusion(f32[2,64,12,2048]{3,1,2,0:T(8,128)S(1)} %fusion.12, bf16[64,2,12,384]{3,0,2,1:T(8,128)(2,1)} %get-tuple-element.14, bf16[2,2048,384]{2,1,0:T(8,128)(2,1)S(1)} %copy-done.7), kind=kOutput, calls=%fused_computation.9 | convolution fusion | flops 2419064832 | bytes 29491200 | tf_op jit(solution)/shard_map/slch,ldh->slcd/dot_general | solution.py:78
  240.6 16.4 %copy.41 = f32[64,24,2048]{2,1,0:T(8,128)} copy(f32[64,24,2048]{2,0,1:T(8,128)} %bitcast.128) | data formatting | bytes 25165824 | tf_op jit(solution)/shard_map/reshape | solution.py:79
  257.1 8.0 %fusion.18 = f32[2,64,12,2048]{3,1,2,0:T(8,128)} fusion(bf16[64,2,12,384]{3,0,2,1:T(8,128)(2,1)} %get-tuple-element.16, bf16[2,384,2048]{2,1,0:T(8,128)(2,1)S(1)} %copy-done), kind=kOutput, calls=%fused_computation.28 | convolution fusion | flops 2415919104 | bytes 16908288 | tf_op jit(solution)/shard_map/slch,lhd->slcd/dot_general | solution.py:48
  265.1 16.3 %copy.36 = f32[64,24,2048]{2,1,0:T(8,128)} copy(f32[64,24,2048]{2,0,1:T(8,128)} %bitcast.127) | data formatting | bytes 25165824 | tf_op jit(solution)/shard_map/reshape | solution.py:49
  281.5 126.2 %reduce-scatter.5.cloned.1.call-done = f32[64,24,1024]{2,1,0:T(8,128)} async-done(((f32[64,24,2048]{2,1,0:T(8,128)}), f32[64,24,1024]{2,1,0:T(8,128)}) %reduce-scatter.5.cloned.1.call-update) | async-done | bytes 6291472 | tf_op jit(solution)/shard_map/reduce_scatter | solution.py:33
  407.7 4.9 convert_element_type.79
  412.6 9.9 %all-to-all-start.4 = ((bf16[64,24,1024]{2,1,0:T(8,128)(2,1)}), bf16[64,24,1024]{2,1,0:T(8,128)(2,1)S(1)}, u32[]{:S(2)}, u32[]{:S(2)}) async-start(bf16[64,24,1024]{2,1,0:T(8,128)(2,1)} %convert_element_type.79), calls=%async_computation.6 | async-start | bytes 6291456 | tf_op jit(solution)/shard_map/all_to_all | solution.py:36
  422.6 0.9 convert_element_type.80
  423.5 170.8 %reduce-scatter.3.cloned.1.call-done = f32[64,24,1024]{2,1,0:T(8,128)} async-done(((f32[64,24,2048]{2,1,0:T(8,128)}), f32[64,24,1024]{2,1,0:T(8,128)}) %reduce-scatter.3.cloned.1.call-update) | async-done | bytes 6291472 | tf_op jit(solution)/shard_map/reduce_scatter | solution.py:33
  594.2 4.9 convert_element_type.69
  599.1 7.9 %all-to-all-start.1 = ((bf16[64,24,1024]{2,1,0:T(8,128)(2,1)}), bf16[64,24,1024]{2,1,0:T(8,128)(2,1)}, u32[]{:S(2)}, u32[]{:S(2)}) async-start(bf16[64,24,1024]{2,1,0:T(8,128)(2,1)} %convert_element_type.69), calls=%async_computation.2 | async-start | bytes 6291456 | tf_op jit(solution)/shard_map/all_to_all | solution.py:36
  607.1 7.6 %bitcast_convert_fusion = bf16[2,384,2048]{2,1,0:T(8,128)(2,1)} fusion(bf16[64,2,12,384]{3,0,2,1:T(8,128)(2,1)} %get-tuple-element.16, bf16[64,2,12,2048]{3,0,2,1:T(8,128)(2,1)} %bitcast.138), kind=kOutput, calls=%fused_computation.6 | convolution fusion | flops 2417491968 | bytes 10616832 | tf_op jit(solution)/shard_map/slch,slcd->lhd/dot_general | solution.py:62
  614.7 8.1 %bitcast_convert_fusion.1 = bf16[2,2048,384]{2,1,0:T(8,128)(2,1)} fusion(bf16[64,2,12,2048]{3,0,2,1:T(8,128)(2,1)} %bitcast.133, bf16[64,2,12,384]{3,0,2,1:T(8,128)(2,1)S(1)} %copy-done.10), kind=kOutput, calls=%fused_computation.7 | convolution fusion | flops 2417491968 | bytes 10616832 | tf_op jit(solution)/shard_map/slcd,slch->ldh/dot_general | solution.py:73
  622.8 4.9 bitcast_convert_fusion.2
  627.7 5.4 gather_fusion.1
  633.1 3.7 bitcast_reduce_fusion
  636.8 11.5 %all-to-all-done.1 = bf16[64,24,1024]{2,1,0:T(8,128)(2,1)} async-done(((bf16[64,24,1024]{2,1,0:T(8,128)(2,1)}), bf16[64,24,1024]{2,1,0:T(8,128)(2,1)}, u32[]{:S(2)}, u32[]{:S(2)}) %all-to-all-start.1) | async-done | bytes 3145760 | tf_op jit(solution)/shard_map/all_to_all | solution.py:36
  648.3 8.5 %gather_fusion = bf16[1024,1024]{1,0:T(8,128)(2,1)} fusion(bf16[1536,1024]{1,0:T(8,128)(2,1)} %bitcast.18, s32[1024]{0:T(1024)S(1)} %broadcast_clamp_fusion), kind=kCustom, calls=%fused_computation | custom fusion | bytes 4198400 | tf_op jit(solution)/shard_map/gather | solution.py:37
  656.8 4.1 fusion.2
  660.8 9.5 %psum.7 = f32[128,8]{1,0:T(8,128)S(1)} all-reduce(f32[128,8]{1,0:T(8,128)S(1)} %get-tuple-element.12), channel_id=1, replica_groups=mesh['dp'=64,'col'=2] {'col'}, use_global_device_ids=true, to_apply=%region_10.11 | all-reduce | flops 1024 | bytes 8192 | tf_op jit(solution)/shard_map/psum | solution.py:81
  670.4 0.7 copy.42
  (49 shorter events, 0.7 us)
Async XLA Ops:
  7.2 214.7 %copy-start = (bf16[2,384,2048]{2,1,0:T(8,128)(2,1)S(1)}, bf16[2,384,2048]{2,1,0:T(8,128)(2,1)}, u32[]{:S(2)}) copy-start(bf16[2,384,2048]{2,1,0:T(8,128)(2,1)} %param.12) | copy-start | bytes 9437188
  9.3 19.8 %all-to-all-start.2 = ((bf16[2,128,1024]{1,2,0:T(8,128)(2,1)}), bf16[2,128,1024]{1,2,0:T(8,128)(2,1)}, u32[]{:S(2)}, u32[]{:S(2)}) async-start(bf16[2,128,1024]{1,2,0:T(8,128)(2,1)} %pad_maximum_fusion), calls=%async_computation.3 | async-start | bytes 1048576 | tf_op jit(solution)/shard_map/all_to_all | solution.py:55
  15.9 0.8 copy-start.8
  29.1 11.8 %copy-start.12 = (f32[128,8]{0,1:T(8,128)S(1)}, f32[128,8]{0,1:T(8,128)}, u32[]{:S(2)}) copy-start(f32[128,8]{0,1:T(8,128)} %param.9) | copy-start | bytes 12292
  29.1 94.5 %all-to-all-start = ((bf16[64,24,2048]{2,1,0:T(8,128)(2,1)}), bf16[64,24,2048]{2,1,0:T(8,128)(2,1)}, u32[]{:S(2)}, u32[]{:S(2)}) async-start(bf16[64,24,2048]{2,1,0:T(8,128)(2,1)} %bitcast.129), calls=%async_computation | async-start | bytes 12582912 | tf_op jit(solution)/shard_map/all_to_all | solution.py:28
  123.6 91.9 %all-to-all-start.3 = ((bf16[64,24,2048]{2,1,0:T(8,128)(2,1)}), bf16[64,24,2048]{2,1,0:T(8,128)(2,1)}, u32[]{:S(2)}, u32[]{:S(2)}) async-start(bf16[64,24,2048]{2,1,0:T(8,128)(2,1)} %bitcast.130), calls=%async_computation.4 | async-start | bytes 12582912 | tf_op jit(solution)/shard_map/all_to_all | solution.py:28
  132.4 275.3 %reduce-scatter.5.cloned.1.call-start = ((), (), s32[]{:S(2)}) async-start(), calls=%async_computation.8 | async-start | bytes 18874368 | tf_op jit(solution)/shard_map/reduce_scatter | solution.py:33
  132.6 6.4 copy-start.6
  139.0 4.8 copy-start.2
  139.1 4.8 copy-start.4
  215.5 6.4 copy-start.13
  215.5 6.4 copy-start.14
  221.8 6.1 copy-start.3
  221.9 6.0 copy-start.5
  227.9 4.9 copy-start.7
  257.0 337.2 %reduce-scatter.3.cloned.1.call-start = ((), (), s32[]{:S(2)}) async-start(), calls=%async_computation.7 | async-start | bytes 18874368 | tf_op jit(solution)/shard_map/reduce_scatter | solution.py:33
  412.6 9.9 %copy-start.11 = (bf16[128,1024]{1,0:T(8,128)(2,1)S(1)}, bf16[128,1024]{1,0:T(8,128)(2,1)}, u32[]{:S(2)}) copy-start(bf16[128,1024]{1,0:T(8,128)(2,1)} %param.13) | copy-start | bytes 786436
  412.6 186.5 %all-to-all-start.4 = ((bf16[64,24,1024]{2,1,0:T(8,128)(2,1)}), bf16[64,24,1024]{2,1,0:T(8,128)(2,1)S(1)}, u32[]{:S(2)}, u32[]{:S(2)}) async-start(bf16[64,24,1024]{2,1,0:T(8,128)(2,1)} %convert_element_type.79), calls=%async_computation.6 | async-start | bytes 6291456 | tf_op jit(solution)/shard_map/all_to_all | solution.py:36
  599.1 49.2 %all-to-all-start.1 = ((bf16[64,24,1024]{2,1,0:T(8,128)(2,1)}), bf16[64,24,1024]{2,1,0:T(8,128)(2,1)}, u32[]{:S(2)}, u32[]{:S(2)}) async-start(bf16[64,24,1024]{2,1,0:T(8,128)(2,1)} %convert_element_type.69), calls=%async_computation.2 | async-start | bytes 6291456 | tf_op jit(solution)/shard_map/all_to_all | solution.py:36
  607.1 7.6 %copy-start.10 = (bf16[64,2,12,384]{3,0,2,1:T(8,128)(2,1)S(1)}, bf16[64,2,12,384]{3,0,2,1:T(8,128)(2,1)}, u32[]{:S(2)}) copy-start(bf16[64,2,12,384]{3,0,2,1:T(8,128)(2,1)} %get-tuple-element.14) | copy-start | bytes 3538948
  607.1 15.7 %slice-start = ((s8[6291456]{0:T(1024)(128)(4,1)}), s8[4194304]{0:T(1024)(128)(4,1)S(1)}, s32[]{:S(2)}) async-start(s8[6291456]{0:T(1024)(128)(4,1)} %bitcast.134), calls=%async_computation.9 | async-start | bytes 8388608
  614.7 8.1 %slice-start.1 = ((s8[6291456]{0:T(1024)(128)(4,1)}), s8[2097152]{0:T(1024)(128)(4,1)S(1)}, s32[]{:S(2)}) async-start(s8[6291456]{0:T(1024)(128)(4,1)} %bitcast.134), calls=%async_computation.10 | async-start | bytes 4194304
  614.7 8.1 %copy-start.9 = (bf16[64,2,12,384]{3,0,2,1:T(8,128)(2,1)S(1)}, bf16[64,2,12,384]{3,0,2,1:T(8,128)(2,1)}, u32[]{:S(2)}) copy-start(bf16[64,2,12,384]{3,0,2,1:T(8,128)(2,1)} %get-tuple-element.15) | copy-start | bytes 3538948
  648.3 22.8 %copy-start.1 = (bf16[2,384,2048]{2,1,0:T(8,128)(2,1)S(1)}, bf16[2,384,2048]{2,1,0:T(8,128)(2,1)}, u32[]{:S(2)}) copy-start(bf16[2,384,2048]{2,1,0:T(8,128)(2,1)} %param.12) | copy-start | bytes 9437188
Sparse Core Ops, SparseCore 0:
  257.1 150.4 reduce-scatter.4
  410.1 184.0 reduce-scatter.2
